TPU v7x, 256 devices: a whole 4x4x8 slice. The times are simulated.
256 devices in a mesh: dp: 32 (over y, x, core), tensor: 8 (over z).
Axes of the slice: x: 4, y: 4, z: 8, core: 2. Of those that a mesh axis runs over, the one named last changes fastest.
Arguments:
- rank_query: bfloat16 [256, 32, 5120], P('dp', None, 'tensor'), may hold values from -4.5 to 4.5
- rank_key: bfloat16 [256, 32, 5120], P('dp', None, 'tensor'), may hold values from -4.5 to 4.5
- rank_value: bfloat16 [256, 32, 5120], P('dp', None, 'tensor'), may hold values from -6 to 6
- rank_resid: bfloat16 [256, 32, 5120], P(('dp', 'tensor')), may hold values from -4 to 4
- out_weight: bfloat16 [5120, 5120], P('tensor', 'dp'), may hold values from -0.25 to 0.25
- rank_gain: bfloat16 [5120], replicated, may hold values from 0.099609375 to 1.8984375
- score_weight: bfloat16 [5120], replicated, may hold values from -0.078125 to 0.078125
- pair_index: int32 [256, 3], P(('dp', 'tensor')), may hold values from 0 to 31, as said below
- cand_rank: int32 [1024, 8], P('dp'), may hold values from 0 to 7, each once within a row
- cand_len: int32 [1024, 8], P('dp'), may hold values from 1 to 8, 39 in all within a row
- blend_owner: int32 [32, 32], P('dp'), may hold values from 0 to 31, each once within a row
- blend_rows: bfloat16 [1024, 8, 8, 4096], P('dp', None, None, 'tensor'), may hold values from -6 to 6
- blend_gain: bfloat16 [4096], replicated, may hold values from 0.099609375 to 1.8984375
- blend_weight: bfloat16 [4096, 3, 2048], P('dp', None, 'tensor'), may hold values from -0.09375 to 0.09375
Outputs:
- rank_hidden: bfloat16 [256, 32, 5120], P(('dp', 'tensor'))
- cand_score: float32 [1024, 8], P('dp')
- blended_qkv: bfloat16 [1024, 24, 3, 2048], P('dp', None, None, 'tensor')
Inputs may be any that keep to these rules, and one draw needn't show every extreme that they name: `pair_index`: column 0 is a prompt of the pair's own group of 32 prompts (pair p belongs to group p // 8); columns 1 and 2 are two different candidates of that prompt. `cand_rank`: each row gives every rank once. `blend_owner`: each row names every group once.
All inputs are finite; a program needn't handle non-finite values.
Results may differ from a plain program's by a relative error of at most 0.024.
Values may be sent and summed in bfloat16 or wider, within the bound.
No kernel may reach another device: no remote copies, remote signals or barrier semaphores. Data moves between devices by JAX's collectives and lax.ppermute only.
A program may use at most 128 MiB of HBM per device.

v0:
```python
import math
import jax
import jax.numpy as jnp
from jax import lax
from jax.sharding import PartitionSpec as P

HR = 40
HDR = 128


def pair_attention(queries, keys_in, values_in, head_count):
    pair_count, length, row_width = queries.shape
    head_size = row_width // head_count
    query_heads = queries.reshape(pair_count, length, head_count, head_size)
    key_heads = keys_in.reshape(pair_count, length, head_count, head_size)
    value_heads = values_in.reshape(pair_count, length, head_count, head_size)
    scores = jnp.einsum(
        "pihd,pjhd->phij", query_heads, key_heads, preferred_element_type=jnp.float32
    ) * (1.0 / math.sqrt(HDR))
    highest = jnp.max(scores, axis=-1, keepdims=True)
    weights = jnp.exp(scores - highest)
    soft_weights = (weights / jnp.sum(weights, axis=-1, keepdims=True)).astype(jnp.bfloat16)
    context = jnp.einsum(
        "phij,pjhd->pihd", soft_weights, value_heads, preferred_element_type=jnp.float32
    )
    return context.astype(jnp.bfloat16).reshape(pair_count * length, row_width)


def encode(rows_in, blend_gain, blend_weight):
    whole_rows = lax.all_gather(rows_in, "tensor", axis=3, tiled=True)
    prompts, pick_count, length, features = whole_rows.shape
    flat_rows = whole_rows.reshape(prompts * pick_count * length, features)
    as_float = flat_rows.astype(jnp.float32)
    scale_rows = lax.rsqrt(jnp.mean(as_float * as_float, axis=-1, keepdims=True) + 1e-06)
    blend_normed = (as_float * scale_rows * blend_gain.astype(jnp.float32)).astype(jnp.bfloat16)
    columns = blend_weight.shape[1] * blend_weight.shape[2]
    portion = lax.all_gather(blend_weight, "dp", axis=0, tiled=True)
    projected = jnp.dot(
        blend_normed, portion.reshape(portion.shape[0], columns), preferred_element_type=jnp.float32
    )
    return projected.astype(jnp.bfloat16).reshape(
        prompts, pick_count * length, blend_weight.shape[1], blend_weight.shape[2]
    )


def body(
    rank_query,
    rank_key,
    rank_value,
    rank_resid,
    out_weight,
    rank_gain,
    score_weight,
    pair_index,
    cand_rank,
    cand_len,
    blend_owner,
    blend_rows,
    blend_gain,
    blend_weight,
):
    tensor_count = lax.axis_size("tensor")
    local_heads = HR // tensor_count
    length = rank_query.shape[1]
    context = pair_attention(rank_query, rank_key, rank_value, local_heads)
    own_pairs = rank_resid.shape[0]
    own_rows = own_pairs * length
    term_rows = jnp.dot(
        context,
        lax.all_gather(out_weight, "dp", axis=1, tiled=True),
        preferred_element_type=jnp.float32,
    )
    summed = lax.psum(term_rows.astype(jnp.bfloat16), "tensor").astype(jnp.float32)
    part_sum = lax.dynamic_slice_in_dim(summed, lax.axis_index("tensor") * own_rows, own_rows, 0)
    mixed_rows = rank_resid.reshape(own_rows, -1).astype(jnp.float32) + part_sum
    mean_square = jnp.mean(mixed_rows * mixed_rows, axis=-1, keepdims=True)
    normed = mixed_rows * lax.rsqrt(mean_square + 1e-05) * rank_gain.astype(jnp.float32)
    rank_hidden = normed.astype(jnp.bfloat16).reshape(rank_resid.shape)
    leading = normed.reshape(own_pairs, length, -1)[:, 0, :]
    pair_logit = jnp.sum(leading * score_weight.astype(jnp.float32), axis=-1)
    prompt_count = cand_rank.shape[0]
    cand_count = cand_rank.shape[1]
    slot_ids = jnp.arange(prompt_count * cand_count, dtype=jnp.int32)
    base_slot = pair_index[:, 0] * cand_count
    upward = jnp.where(
        (base_slot + pair_index[:, 1])[:, None] == slot_ids[None, :], pair_logit[:, None], 0.0
    )
    downward = jnp.where(
        (base_slot + pair_index[:, 2])[:, None] == slot_ids[None, :], pair_logit[:, None], 0.0
    )
    vote_sums = jnp.sum(upward - downward, axis=0).reshape(prompt_count, cand_count)
    cand_score = lax.psum(vote_sums, "tensor")
    places = jnp.arange(3, dtype=jnp.int32)
    matched = cand_rank[:, None, :] == places[None, :, None]
    labels = jnp.arange(cand_count, dtype=jnp.int32)
    chosen = jnp.sum(jnp.where(matched, labels[None, None, :], 0), axis=-1)
    chosen_len = jnp.sum(jnp.where(matched, cand_len[:, None, :], 0), axis=-1)
    prompt_ids = jnp.arange(prompt_count, dtype=jnp.int32)
    picked = blend_rows[prompt_ids[:, None], chosen]
    positions = jnp.arange(blend_rows.shape[2], dtype=jnp.int32)
    live_rows = positions[None, None, :] < chosen_len[:, :, None]
    picked = jnp.where(live_rows[..., None], picked, jnp.zeros((), jnp.bfloat16))
    owners = blend_owner[0]
    sender = jnp.sum(
        jnp.where(owners[None, :] == prompt_ids[:, None], prompt_ids[None, :], 0), axis=1
    )
    outgoing = picked[sender]
    arrived = lax.all_to_all(outgoing, "dp", split_axis=0, concat_axis=0, tiled=True)
    blended_qkv = encode(arrived, blend_gain, blend_weight)
    return (rank_hidden, cand_score, blended_qkv)


def solution(mesh):
    placed = (
        P("dp", None, "tensor"),
        P("dp", None, "tensor"),
        P("dp", None, "tensor"),
        P(("dp", "tensor"), None, None),
        P("tensor", "dp"),
        P(),
        P(),
        P(("dp", "tensor"), None),
        P("dp", None),
        P("dp", None),
        P("dp", None),
        P("dp", None, None, "tensor"),
        P(),
        P("dp", None, "tensor"),
    )
    return jax.shard_map(
        body,
        mesh=mesh,
        in_specs=placed,
        out_specs=(P(("dp", "tensor"), None, None), P("dp", None), P("dp", None, None, "tensor")),
        check_vma=False,
    )
```

profile of v0, /device:TPU:2, one launch (start us, length us, event | category | flops | bytes accessed | tf_op | source)
XLA Modules:
  0.0 343.9 jit_solution(1360914309973684097)
XLA Ops:
  7.2 0.0 copy-start
  7.2 0.0 copy-start.3
  7.2 0.0 copy-start.2
  7.2 0.0 all-gather.6.cloned.1.call-start
  7.2 0.9 select_reduce_fusion.2
  8.1 0.1 copy.60
  8.2 0.1 reshape.142
  8.3 0.1 copy.59
  8.4 0.1 iota_compare_fusion
  8.5 0.8 select_reduce_fusion
  9.3 0.6 pad_clamp_fusion
  9.9 2.0 gather_fusion
  11.9 1.3 broadcast_select_fusion
  13.3 0.0 copy-start.5
  13.3 0.0 copy-start.6
  13.3 1.7 gather_fusion.1
  15.0 21.0 %all_to_all.5 = bf16[32,3,8,512]{3,2,1,0:T(8,128)(2,1)} all-to-all(bf16[32,3,8,512]{3,2,1,0:T(8,128)(2,1)} %gather_fusion.1), channel_id=1, replica_groups=mesh['dp'=32,'tensor'=8] {'dp'}, dimensions={0} | all-to-all | bytes 1572864 | tf_op jit(solution)/shard_map/all_to_all | solution.py:108
  36.0 0.0 all-gather.6.cloned.1.call-update
  36.1 0.0 all-gather.4.cloned.1.call-start
  36.1 0.7 all-gather.4.cloned.1.call-update
  36.8 0.0 all-gather.8.cloned.1.call-start
  36.9 1.7 copy.63
  38.6 0.0 all-gather.8.cloned.1.call-update
  38.6 0.0 all-reduce.2.cloned.1.call-start
  38.7 1.0 fusion.32
  39.7 0.3 convolution_multiply_fusion
  40.0 1.3 fusion.6
  41.3 0.2 copy.58
  41.5 0.6 fusion.31
  44.0 0.7 convert_element_type.58
  44.7 66.2 %all-gather.6.cloned.1.call-done = bf16[32,3,8,4096]{3,2,1,0:T(8,128)(2,1)} async-done(((bf16[32,3,8,512]{3,2,1,0:T(8,128)(2,1)}), bf16[32,3,8,4096]{3,2,1,0:T(8,128)(2,1)}) %all-gather.6.cloned.1.call-update) | async-done | bytes 6291472 | tf_op jit(solution)/shard_map/all_gather | solution.py:30
  110.9 4.1 %fusion.1 = f32[32,3,8]{2,1,0:T(4,128)S(1)} fusion(bf16[32,3,8,4096]{3,2,1,0:T(8,128)(2,1)} %all-gather.6.cloned.1.call-done), kind=kLoop, calls=%fused_computation.5 | loop fusion | flops 9436416 | bytes 6294528 | tf_op jit(solution)/shard_map/reduce_sum | solution.py:34
  115.0 0.1 copy.61
  115.1 0.1 copy.62
  115.2 50.6 %all-gather.4.cloned.1.call-done = bf16[640,5120]{0,1:T(8,128)(2,1)} async-done(((bf16[640,160]{0,1:T(8,128)(2,1)}), bf16[640,5120]{0,1:T(8,128)(2,1)}) %all-gather.4.cloned.1.call-update) | async-done | bytes 6553616 | tf_op jit(solution)/shard_map/all_gather | solution.py:70
  165.7 6.6 %convolution_convert_fusion = bf16[256,5120]{1,0:T(8,128)(2,1)} fusion(bf16[640,5120]{0,1:T(8,128)(2,1)} %all-gather.4.cloned.1.call-done, bf16[32,8,5,128]{3,2,1,0:T(8,128)(2,1)S(1)} %bitcast.74), kind=kOutput, calls=%fused_computation.8 | convolution fusion | flops 1679032320 | bytes 9502720 | tf_op jit(solution)/shard_map/dot_general | solution.py:68
  172.3 0.0 all-reduce.2.cloned.1.call-update
  172.4 8.2 %fusion.3 = bf16[32,3,8,4096]{3,2,1,0:T(8,128)(2,1)} fusion(bf16[32,3,8,4096]{3,2,1,0:T(8,128)(2,1)} %all-gather.6.cloned.1.call-done, f32[4096]{0:T(1024)S(1)} %convert_element_type.58, f32[32,3,8]{2,1,0:T(4,128)S(1)} %copy.62), kind=kLoop, calls=%fused_computation.7 | loop fusion | flops 12582912 | bytes 12602368 | tf_op jit(solution)/shard_map/convert_element_type | solution.py:35
  180.5 47.1 %all-gather.8.cloned.1.call-done = bf16[4096,3,256]{0,2,1:T(8,128)(2,1)} async-done(((bf16[128,3,256]{0,2,1:T(8,128)(2,1)}), bf16[4096,3,256]{0,2,1:T(8,128)(2,1)}) %all-gather.8.cloned.1.call-update) | async-done | bytes 6291472 | tf_op jit(solution)/shard_map/all_gather | solution.py:37
  227.7 9.9 %convolution_convert_fusion.1 = bf16[768,768]{1,0:T(8,128)(2,1)} fusion(bf16[768,4096]{1,0:T(8,128)(2,1)} %bitcast.72, bf16[4096,768]{0,1:T(8,128)(2,1)} %bitcast.76), kind=kOutput, calls=%fused_computation.9 | convolution fusion | flops 4832428032 | bytes 13762560 | tf_op jit(solution)/shard_map/dot_general | solution.py:38
  237.6 3.7 %reshape.140 = bf16[32,24,3,256]{3,2,1,0:T(4,128)(2,1)} reshape(bf16[768,768]{1,0:T(8,128)(2,1)} %convolution_convert_fusion.1) | data formatting | bytes 2359296 | tf_op jit(solution)/shard_map/reshape | solution.py:41
  241.3 2.6 copy.64
  243.9 72.1 %all-reduce.2.cloned.1.call-done = bf16[256,5120]{1,0:T(8,128)(2,1)} async-done(((bf16[256,5120]{1,0:T(8,128)(2,1)}), bf16[256,5120]{1,0:T(8,128)(2,1)}) %all-reduce.2.cloned.1.call-update) | async-done | bytes 2621456 | tf_op jit(solution)/shard_map/psum | solution.py:73
  316.0 1.2 multiply_reduce_fusion
  317.2 1.8 fusion.7
  319.1 0.6 multiply_reduce_fusion.1
  319.7 0.6 select_subtract_fusion
  320.2 17.1 %psum.15 = f32[32,8]{0,1:T(8,128)} all-reduce(f32[32,8]{0,1:T(8,128)S(1)} %select_subtract_fusion), channel_id=1, replica_groups=mesh['dp'=32,'tensor'=8] {'tensor'}, use_global_device_ids=true, to_apply=%region_5.6 | all-reduce | flops 256 | bytes 2048 | tf_op jit(solution)/shard_map/psum | solution.py:92
  (15 shorter events, 0.1 us)
Async XLA Ops:
  7.2 2.7 copy-start
  7.2 31.5 %copy-start.3 = (bf16[8,32,640]{2,1,0:T(8,128)(2,1)S(1)}, bf16[8,32,640]{2,1,0:T(8,128)(2,1)}, u32[]{:S(2)}) copy-start(bf16[8,32,640]{2,1,0:T(8,128)(2,1)} %param.14) | copy-start | bytes 983044
  7.2 31.5 %copy-start.2 = (bf16[8,32,640]{2,1,0:T(8,128)(2,1)S(1)}, bf16[8,32,640]{2,1,0:T(8,128)(2,1)}, u32[]{:S(2)}) copy-start(bf16[8,32,640]{2,1,0:T(8,128)(2,1)} %param.15) | copy-start | bytes 983044
  7.2 103.7 %all-gather.6.cloned.1.call-start = ((), (), s32[]{:S(2)}) async-start(), calls=%async_computation.3 | async-start | bytes 7077888 | tf_op jit(solution)/shard_map/all_gather | solution.py:30
  13.3 28.3 %copy-start.5 = (bf16[5120]{0:T(1024)(128)(2,1)S(1)}, bf16[5120]{0:T(1024)(128)(2,1)}, u32[]{:S(2)}) copy-start(bf16[5120]{0:T(1024)(128)(2,1)} %param.19) | copy-start | bytes 30724
  13.3 28.3 %copy-start.6 = (s32[1,3]{1,0:T(1,128)S(1)}, s32[1,3]{1,0:T(1,128)}, u32[]{:S(2)}) copy-start(s32[1,3]{1,0:T(1,128)} %param.21) | copy-start | bytes 40
  36.1 129.7 %all-gather.4.cloned.1.call-start = ((), (), s32[]{:S(2)}) async-start(), calls=%async_computation.1 | async-start | bytes 6758400 | tf_op jit(solution)/shard_map/all_gather | solution.py:70
  36.8 190.9 %all-gather.8.cloned.1.call-start = ((), (), s32[]{:S(2)}) async-start(), calls=%async_computation.4 | async-start | bytes 6488064 | tf_op jit(solution)/shard_map/all_gather | solution.py:37
  38.6 277.4 %all-reduce.2.cloned.1.call-start = ((), (), s32[]{:S(2)}) async-start(), calls=%async_computation.2 | async-start | bytes 5242880 | tf_op jit(solution)/shard_map/psum | solution.py:73
  227.7 88.3 %copy-start.1 = (bf16[1,32,5120]{2,1,0:T(8,128)(2,1)S(1)}, bf16[1,32,5120]{2,1,0:T(8,128)(2,1)}, u32[]{:S(2)}) copy-start(bf16[1,32,5120]{2,1,0:T(8,128)(2,1)} %param.17) | copy-start | bytes 983044
  237.6 81.5 %copy-start.4 = (bf16[5120]{0:T(1024)(128)(2,1)S(1)}, bf16[5120]{0:T(1024)(128)(2,1)}, u32[]{:S(2)}) copy-start(bf16[5120]{0:T(1024)(128)(2,1)} %param.20) | copy-start | bytes 30724
Sparse Core Ops, SparseCore 0:
  36.2 74.6 all-gather.5
  113.4 52.2 all-gather.3
  168.8 58.8 all-gather.7
  229.9 86.0 all-reduce.1
where the time goes:
time: 345 us; the launch traced here: 344 us
  waiting for transfers between devices  237 us (69%)
  blocking collectives  38.1 us (11%)
  other arithmetic  20.9 us (6%)
  matrix products  19.1 us (6%)
  between operations  15.8 us (5%)
  local copies, waits for them, and re-layouts  13.1 us (4%)
    psum x1, waiting for transfers between devices, body(): lax.psum(term_rows.astype(jnp.bfloat16), 'tensor').astype(jnp.float32)  72.1 us
    all_gather x1, waiting for transfers between devices, encode(): whole_rows = lax.all_gather(rows_in, 'tensor', axis=3, tiled=True)  66.2 us
    all_gather x1, waiting for transfers between devices, body(): lax.all_gather(out_weight, 'dp', axis=1, tiled=True)  50.6 us
    all_gather x1, waiting for transfers between devices, encode(): portion = lax.all_gather(blend_weight, 'dp', axis=0, tiled=True)  47.1 us
    all_to_all x1, blocking collectives, body(): lax.all_to_all(outgoing, 'dp', split_axis=0, concat_axis=0, tiled=True)  21 us
    psum x1, blocking collectives, body(): cand_score = lax.psum(vote_sums, 'tensor')  17.1 us
    dot_general x1, matrix products, encode(): jnp.dot(blend_normed, portion.reshape(portion.shape[0], columns), preferr...  9.89 us
    convert_element_type x1, other arithmetic, encode(): (as_float * scale_rows * blend_gain.astype(jnp.float32)).astype(jnp.bfloa...  8.16 us
  transfers between devices with their start and end apart: 4, of which 4 were waited for; matrix products, arithmetic and copies ran while one was open for 12% of the time, Pallas kernels for 0%

commit v1 on v0

--- a/solution.py
+++ b/solution.py
@@ -6,6 +6,14 @@
 
 HR = 40
 HDR = 128
+
+
+def tiled_gather(value, axis, dim):
+    count = lax.axis_size(axis)
+    repeats = [count if d == dim else 1 for d in range(value.ndim)]
+    return lax.all_to_all(
+        jnp.tile(value, repeats), axis, split_axis=dim, concat_axis=dim, tiled=True
+    )
 
 
 def pair_attention(queries, keys_in, values_in, head_count):
@@ -66,9 +74,7 @@
     own_pairs = rank_resid.shape[0]
     own_rows = own_pairs * length
     term_rows = jnp.dot(
-        context,
-        lax.all_gather(out_weight, "dp", axis=1, tiled=True),
-        preferred_element_type=jnp.float32,
+        context, tiled_gather(out_weight, "dp", 1), preferred_element_type=jnp.float32
     )
     summed = lax.psum(term_rows.astype(jnp.bfloat16), "tensor").astype(jnp.float32)
     part_sum = lax.dynamic_slice_in_dim(summed, lax.axis_index("tensor") * own_rows, own_rows, 0)

time: 345 us -> 349 us (1.012)
  starting transfers between devices: 0.16 us -> 7.92 us
    all_to_all x0 -> x1, waiting for transfers between devices: none -> 75.9 us  [tiled_gather(): lax.all_to_all(jnp.tile(value, repeats), axis, split_axis=dim, concat_axi...]
    all_gather x1 -> x0, waiting for transfers between devices: 50.6 us -> none  [body(): lax.all_gather(out_weight, 'dp', axis=1, tiled=True)]
    psum x1, waiting for transfers between devices: 72.1 us -> 59.1 us  [body(): lax.psum(term_rows.astype(jnp.bfloat16), 'tensor').astype(jnp.float32)]
    all_gather x1, waiting for transfers between devices: 66.2 us -> 53.2 us  [encode(): whole_rows = lax.all_gather(rows_in, 'tensor', axis=3, tiled=True)]
    all_to_all x0 -> x1, starting transfers between devices: none -> 7.8 us  [tiled_gather(): lax.all_to_all(jnp.tile(value, repeats), axis, split_axis=dim, concat_axi...]
    another operation x0 -> x1, local copies, waits for them, and re-layouts: none -> 4.28 us  [tiled_gather(): jnp.tile(value, repeats)]
  transfers between devices with their start and end apart: 4 -> 4, of which waited for: 4 -> 4; matrix products, arithmetic and copies ran while one was open for 12% -> 7% of each run, Pallas kernels for 0% -> 0%
where the time goes in v1:
time: 349 us; the launch traced here: 347 us
  waiting for transfers between devices  237 us (68%)
  blocking collectives  37.8 us (11%)
  other arithmetic  17.9 us (5%)
  matrix products  17.6 us (5%)
  between operations  15.9 us (5%)
  local copies, waits for them, and re-layouts  13.7 us (4%)
  starting transfers between devices  7.92 us (2%)
    all_to_all x1, waiting for transfers between devices, tiled_gather(): lax.all_to_all(jnp.tile(value, repeats), axis, split_axis=dim, concat_axi...  75.9 us
    psum x1, waiting for transfers between devices, body(): lax.psum(term_rows.astype(jnp.bfloat16), 'tensor').astype(jnp.float32)  59.1 us
    all_gather x1, waiting for transfers between devices, encode(): whole_rows = lax.all_gather(rows_in, 'tensor', axis=3, tiled=True)  53.2 us
    all_gather x1, waiting for transfers between devices, encode(): portion = lax.all_gather(blend_weight, 'dp', axis=0, tiled=True)  48.3 us
    all_to_all x1, blocking collectives, body(): lax.all_to_all(outgoing, 'dp', split_axis=0, concat_axis=0, tiled=True)  20.5 us
    psum x1, blocking collectives, body(): cand_score = lax.psum(vote_sums, 'tensor')  17.4 us
    dot_general x1, matrix products, encode(): jnp.dot(blend_normed, portion.reshape(portion.shape[0], columns), preferr...  9.04 us
    convert_element_type x1, other arithmetic, encode(): (as_float * scale_rows * blend_gain.astype(jnp.float32)).astype(jnp.bfloa...  8.13 us
  transfers between devices with their start and end apart: 4, of which 4 were waited for; matrix products, arithmetic and copies ran while one was open for 7% of the time, Pallas kernels for 0%

profile of v1, /device:TPU:2, one launch (start us, length us, event | category | flops | bytes accessed | tf_op | source)
XLA Modules:
  0.0 347.4 jit_solution(12593809048193711153)
XLA Ops:
  7.2 0.0 copy-start
  7.2 4.3 %tile.2 = bf16[640,32,160]{0,2,1:T(8,128)(2,1)} broadcast(bf16[640,160]{0,1:T(8,128)(2,1)} %param.18), dimensions={0,2} | broadcast | bytes 6758400 | tf_op jit(solution)/shard_map/tile | solution.py:15
  11.5 7.8 %all-to-all-start = ((bf16[640,32,160]{0,2,1:T(8,128)(2,1)}), bf16[640,32,160]{0,2,1:T(8,128)(2,1)}, u32[]{:S(2)}, u32[]{:S(2)}) async-start(bf16[640,32,160]{0,2,1:T(8,128)(2,1)} %tile.2), calls=%async_computation | async-start | bytes 13107200 | tf_op jit(solution)/shard_map/all_to_all | solution.py:14
  19.3 0.0 all-reduce.2.cloned.1.call-start
  19.3 0.0 copy-done.2
  19.3 0.0 copy-done.3
  19.3 0.4 fusion.32
  19.7 0.3 convolution_multiply_fusion
  20.0 1.3 fusion.6
  21.3 0.2 copy.59
  21.5 0.0 copy-start.9
  21.5 0.0 copy-start.10
  21.5 75.9 %all-to-all-done = bf16[640,32,160]{0,2,1:T(8,128)(2,1)} async-done(((bf16[640,32,160]{0,2,1:T(8,128)(2,1)}), bf16[640,32,160]{0,2,1:T(8,128)(2,1)}, u32[]{:S(2)}, u32[]{:S(2)}) %all-to-all-start) | async-done | bytes 6553632 | tf_op jit(solution)/shard_map/all_to_all | solution.py:14
  97.5 6.6 %convolution_convert_fusion = bf16[256,5120]{1,0:T(8,128)(2,1)} fusion(bf16[640,5120]{0,1:T(8,128)(2,1)} %bitcast.2, bf16[32,8,5,128]{3,2,1,0:T(8,128)(2,1)S(1)} %bitcast.75), kind=kOutput, calls=%fused_computation.8 | convolution fusion | flops 1679032320 | bytes 9502720 | tf_op jit(solution)/shard_map/dot_general | solution.py:76
  104.1 0.0 copy-start.1
  104.1 0.0 copy-start.5
  104.1 0.0 all-reduce.2.cloned.1.call-update
  104.1 0.0 all-gather.3.cloned.1.call-start
  104.2 0.1 copy.61
  104.3 0.1 reshape.149
  104.4 0.1 copy.60
  104.5 1.0 gather_fusion
  105.6 0.0 copy-done.11
  105.6 0.1 select_reduce_fusion
  105.7 0.1 iota_compare_fusion
  105.8 1.1 broadcast_select_fusion
  106.9 1.7 gather_fusion.1
  108.6 20.5 %all_to_all.14 = bf16[32,3,8,512]{3,2,1,0:T(8,128)(2,1)} all-to-all(bf16[32,3,8,512]{3,2,1,0:T(8,128)(2,1)S(1)} %gather_fusion.1), channel_id=1, replica_groups=mesh['dp'=32,'tensor'=8] {'dp'}, dimensions={0} | all-to-all | bytes 1572864 | tf_op jit(solution)/shard_map/all_to_all | solution.py:114
  129.1 0.0 all-gather.3.cloned.1.call-update
  129.1 0.0 all-gather.5.cloned.1.call-start
  129.1 0.8 copy.64
  130.0 0.0 all-gather.5.cloned.1.call-update
  130.0 0.6 fusion.31
  132.5 59.1 %all-reduce.2.cloned.1.call-done = bf16[256,5120]{1,0:T(8,128)(2,1)} async-done(((bf16[256,5120]{1,0:T(8,128)(2,1)}), bf16[256,5120]{1,0:T(8,128)(2,1)}) %all-reduce.2.cloned.1.call-update) | async-done | bytes 2621456 | tf_op jit(solution)/shard_map/psum | solution.py:79
  191.6 1.2 multiply_reduce_fusion
  192.8 1.9 fusion.7
  194.7 0.6 multiply_reduce_fusion.1
  195.3 0.6 select_subtract_fusion
  195.9 17.4 %psum.15 = f32[32,8]{0,1:T(8,128)} all-reduce(f32[32,8]{0,1:T(8,128)S(1)} %select_subtract_fusion), channel_id=1, replica_groups=mesh['dp'=32,'tensor'=8] {'tensor'}, use_global_device_ids=true, to_apply=%region_5.6 | all-reduce | flops 256 | bytes 2048 | tf_op jit(solution)/shard_map/psum | solution.py:98
  213.3 53.2 %all-gather.3.cloned.1.call-done = bf16[32,3,8,4096]{3,2,1,0:T(8,128)(2,1)} async-done(((bf16[32,3,8,512]{3,2,1,0:T(8,128)(2,1)}), bf16[32,3,8,4096]{3,2,1,0:T(8,128)(2,1)}) %all-gather.3.cloned.1.call-update) | async-done | bytes 6291472 | tf_op jit(solution)/shard_map/all_gather | solution.py:38
  266.5 4.1 %fusion.1 = f32[32,3,8]{2,1,0:T(4,128)S(1)} fusion(bf16[32,3,8,4096]{3,2,1,0:T(8,128)(2,1)} %all-gather.3.cloned.1.call-done), kind=kLoop, calls=%fused_computation.5 | loop fusion | flops 9436416 | bytes 6294528 | tf_op jit(solution)/shard_map/reduce_sum | solution.py:42
  270.6 0.1 copy.62
  270.7 0.1 copy.63
  270.8 8.1 %fusion.3 = bf16[32,3,8,4096]{3,2,1,0:T(8,128)(2,1)} fusion(bf16[32,3,8,4096]{3,2,1,0:T(8,128)(2,1)} %all-gather.3.cloned.1.call-done, f32[4096]{0:T(1024)S(1)} %convert_element_type.58, f32[32,3,8]{2,1,0:T(4,128)S(1)} %copy.63), kind=kLoop, calls=%fused_computation.7 | loop fusion | flops 12582912 | bytes 12602368 | tf_op jit(solution)/shard_map/convert_element_type | solution.py:43
  279.0 48.3 %all-gather.5.cloned.1.call-done = bf16[4096,3,256]{0,2,1:T(8,128)(2,1)} async-done(((bf16[128,3,256]{0,2,1:T(8,128)(2,1)}), bf16[4096,3,256]{0,2,1:T(8,128)(2,1)}) %all-gather.5.cloned.1.call-update) | async-done | bytes 6291472 | tf_op jit(solution)/shard_map/all_gather | solution.py:45
  327.2 9.0 %convolution_convert_fusion.1 = bf16[768,768]{1,0:T(8,128)(2,1)S(1)} fusion(bf16[768,4096]{1,0:T(8,128)(2,1)} %bitcast.73, bf16[4096,768]{0,1:T(8,128)(2,1)} %bitcast.77), kind=kOutput, calls=%fused_computation.9 | convolution fusion | flops 4832428032 | bytes 13762560 | tf_op jit(solution)/shard_map/dot_general | solution.py:46
  336.3 1.9 reshape.147
  338.2 2.6 copy.65
  (25 shorter events, 0.1 us)
Async XLA Ops:
  7.2 97.4 %copy-start = (bf16[32,8,8,512]{3,2,1,0:T(8,128)(2,1)S(1)}, bf16[32,8,8,512]{3,2,1,0:T(8,128)(2,1)}, u32[]{:S(2)}) copy-start(bf16[32,8,8,512]{3,2,1,0:T(8,128)(2,1)} %param.25) | copy-start | bytes 6291460
  11.5 7.9 %copy-start.2 = (bf16[8,32,640]{2,1,0:T(8,128)(2,1)S(1)}, bf16[8,32,640]{2,1,0:T(8,128)(2,1)}, u32[]{:S(2)}) copy-start(bf16[8,32,640]{2,1,0:T(8,128)(2,1)} %param.15) | copy-start | bytes 983044
  11.5 7.9 %copy-start.3 = (bf16[8,32,640]{2,1,0:T(8,128)(2,1)S(1)}, bf16[8,32,640]{2,1,0:T(8,128)(2,1)}, u32[]{:S(2)}) copy-start(bf16[8,32,640]{2,1,0:T(8,128)(2,1)} %param.14) | copy-start | bytes 983044
  11.5 86.0 %all-to-all-start = ((bf16[640,32,160]{0,2,1:T(8,128)(2,1)}), bf16[640,32,160]{0,2,1:T(8,128)(2,1)}, u32[]{:S(2)}, u32[]{:S(2)}) async-start(bf16[640,32,160]{0,2,1:T(8,128)(2,1)} %tile.2), calls=%async_computation | async-start | bytes 13107200 | tf_op jit(solution)/shard_map/all_to_all | solution.py:14
  19.3 172.3 %all-reduce.2.cloned.1.call-start = ((), (), s32[]{:S(2)}) async-start(), calls=%async_computation.2 | async-start | bytes 5242880 | tf_op jit(solution)/shard_map/psum | solution.py:79
  21.5 82.7 %copy-start.9 = (s32[32,8]{0,1:T(8,128)S(1)}, s32[32,8]{0,1:T(8,128)}, u32[]{:S(2)}) copy-start(s32[32,8]{0,1:T(8,128)} %param.23) | copy-start | bytes 3076
  21.5 82.7 %copy-start.10 = (s32[32,8]{0,1:T(8,128)S(1)}, s32[32,8]{0,1:T(8,128)}, u32[]{:S(2)}) copy-start(s32[32,8]{0,1:T(8,128)} %param.22) | copy-start | bytes 3076
  97.5 8.1 %copy-start.11 = (s32[1,32]{1,0:T(1,128)S(1)}, s32[1,32]{1,0:T(1,128)}, u32[]{:S(2)}) copy-start(s32[1,32]{1,0:T(1,128)} %param.24) | copy-start | bytes 388
  104.1 25.1 %copy-start.4 = (bf16[128,3,256]{2,0,1:T(8,128)(2,1)S(1)}, bf16[128,3,256]{2,0,1:T(8,128)(2,1)}, u32[]{:S(2)}) copy-start(bf16[128,3,256]{2,0,1:T(8,128)(2,1)} %param.27) | copy-start | bytes 589828
  104.1 25.9 %copy-start.6 = (bf16[5120]{0:T(1024)(128)(2,1)S(1)}, bf16[5120]{0:T(1024)(128)(2,1)}, u32[]{:S(2)}) copy-start(bf16[5120]{0:T(1024)(128)(2,1)} %param.19) | copy-start | bytes 30724
  104.1 25.9 %copy-start.8 = (s32[1,3]{1,0:T(1,128)S(1)}, s32[1,3]{1,0:T(1,128)}, u32[]{:S(2)}) copy-start(s32[1,3]{1,0:T(1,128)} %param.21) | copy-start | bytes 40
  104.1 28.4 %copy-start.7 = (bf16[4096]{0:T(1024)(128)(2,1)S(1)}, bf16[4096]{0:T(1024)(128)(2,1)}, u32[]{:S(2)}) copy-start(bf16[4096]{0:T(1024)(128)(2,1)} %param.26) | copy-start | bytes 24580
  104.1 87.5 %copy-start.1 = (bf16[1,32,5120]{2,1,0:T(8,128)(2,1)S(1)}, bf16[1,32,5120]{2,1,0:T(8,128)(2,1)}, u32[]{:S(2)}) copy-start(bf16[1,32,5120]{2,1,0:T(8,128)(2,1)} %param.17) | copy-start | bytes 983044
  104.1 90.6 %copy-start.5 = (bf16[5120]{0:T(1024)(128)(2,1)S(1)}, bf16[5120]{0:T(1024)(128)(2,1)}, u32[]{:S(2)}) copy-start(bf16[5120]{0:T(1024)(128)(2,1)} %param.20) | copy-start | bytes 30724
  104.1 162.4 %all-gather.3.cloned.1.call-start = ((), (), s32[]{:S(2)}) async-start(), calls=%async_computation.3 | async-start | bytes 7077888 | tf_op jit(solution)/shard_map/all_gather | solution.py:38
  129.1 198.2 %all-gather.5.cloned.1.call-start = ((), (), s32[]{:S(2)}) async-start(), calls=%async_computation.4 | async-start | bytes 6488064 | tf_op jit(solution)/shard_map/all_gather | solution.py:45
Sparse Core Ops, SparseCore 0:
  104.3 87.2 all-reduce.1
  193.4 73.1 all-gather.2
  269.6 57.6 all-gather.4
